TPU v7x, 32 devices: a whole 2x2x4 slice. The times are simulated.
32 devices in a mesh: groups: 2 (over x), shard: 16 (over z, y, core).
Axes of the slice: x: 2, y: 2, z: 4, core: 2. Of those that a mesh axis runs over, the one named last changes fastest.
Arguments:
- features: bfloat16 [8192, 4096], P(('groups', 'shard')), parts along dimension 0, may hold values from -6 to 6
- cotangent: bfloat16 [8192, 4096], P(('groups', 'shard')), parts along dimension 0, may hold values from -0.029907227 to 0.029907227
- member_weight: bfloat16 [1024, 4096], P('shard'), may hold values from -0.1875 to 0.1875
- shared_weight: bfloat16 [256, 2048], P('shard'), may hold values from -0.375 to 0.375
- shared_coords: int32 [8, 2], replicated, may hold values from 0 to 15, as said below
Outputs:
- activated: bfloat16 [8192, 4096], P(('groups', 'shard')), parts along dimension 0
- member_grad: float32 [2048, 4096], P(('groups', 'shard')), parts along dimension 0
- shared_grad: float32 [512, 2048], P(('groups', 'shard')), parts along dimension 0
There are 2 independent parts, one for each index of `groups`. A program takes and returns all parts, laid end to end along the dimension named above; an argument that names none is the same for every part. Nothing has to cross between parts.
Inputs may be any that keep to these rules, and one draw needn't show every extreme that they name: `shared_coords`: the 8 pairs (row block, column block) are distinct, and none lies in a member's diagonal square: row block // 4 differs from column block // 4.
All inputs are finite; a program needn't handle non-finite values.
Results may differ from a plain program's by a relative error of at most 0.0029.
Values may be sent and summed in bfloat16 or wider, within the bound.
A program may use at most 128 MiB of HBM per device.

v0:
```python
import jax
import jax.numpy as jnp
from jax import lax
from jax.sharding import PartitionSpec as P

ROOT_HALF = 0.7071067811865476
INV_ROOT_TWO_PI = 0.3989422804014327


def gelu_slope(hidden):
    return 0.5 * (
        1.0 + jax.scipy.special.erf(hidden * ROOT_HALF)
    ) + hidden * INV_ROOT_TWO_PI * jnp.exp(-0.5 * hidden * hidden)


def member_product(inputs, weights):
    return lax.dot_general(
        inputs, weights, (((2,), (0,)), ((1,), (1,))), preferred_element_type=jnp.float32
    )


def per_device(features, cotangent, member_weight, shared_weight, shared_coords):
    shard_count = lax.axis_size("shard")
    token_rows = features.shape[0]
    width = features.shape[1]
    local_rows = member_weight.shape[0]
    member_width = local_rows * shard_count
    members = width // member_width
    block = shared_weight.shape[0] * shard_count
    shared_count = shared_coords.shape[0]
    grid = width // block
    row_blocks = shared_coords[:, 0]
    col_blocks = shared_coords[:, 1]
    col_onehot = (col_blocks[:, None] == jnp.arange(grid, dtype=jnp.int32)[None, :]).astype(
        jnp.float32
    )
    feat_members = features.reshape(token_rows, members, member_width)
    feat_blocks = jnp.take(features.reshape(token_rows, grid, block), row_blocks, axis=1)
    shared_full = lax.all_gather(shared_weight, "shard", axis=0, tiled=True)
    shared_blocks = shared_full.reshape(block, shared_count, block)
    member_full = lax.all_gather(member_weight, "shard", axis=0, tiled=True)
    member_out = member_product(
        feat_members, member_full.reshape(member_width, members, member_width)
    )
    shared_out = lax.dot_general(
        feat_blocks, shared_blocks, (((2,), (0,)), ((1,), (1,))), preferred_element_type=jnp.float32
    )
    placed = jnp.einsum("stj,sk->tkj", shared_out, col_onehot, precision=lax.Precision.HIGHEST)
    hidden = jnp.transpose(member_out, (1, 0, 2)).reshape(token_rows, width) + placed.reshape(
        token_rows, width
    )
    activated = jax.nn.gelu(hidden, approximate=False).astype(jnp.bfloat16)
    grad_hidden = (cotangent.astype(jnp.float32) * gelu_slope(hidden)).astype(jnp.bfloat16)
    grad_members = grad_hidden.reshape(token_rows, members, member_width)
    grad_blocks = jnp.take(grad_hidden.reshape(token_rows, grid, block), col_blocks, axis=1)
    shared_term = lax.dot_general(
        feat_blocks, grad_blocks, (((0,), (0,)), ((1,), (1,))), preferred_element_type=jnp.float32
    )
    shared_term = jnp.transpose(shared_term, (1, 0, 2)).reshape(block, shared_count * block)
    ratio = member_width // block
    folded = shared_term.reshape(member_width, shared_count * block // ratio)
    term = lax.dot_general(
        feat_members, grad_members, (((0,), (0,)), ((1,), (1,))), preferred_element_type=jnp.float32
    )
    joint = lax.psum_scatter(
        jnp.concatenate(
            [
                jnp.transpose(term, (1, 0, 2)).reshape(lax.axis_size("shard") * local_rows, width),
                folded,
            ],
            axis=1,
        ),
        "shard",
        scatter_dimension=0,
        tiled=True,
    )
    member_grad = joint[:, :width]
    shared_grad = joint[:, width:].reshape(local_rows // ratio, shared_count * block)
    return (activated, member_grad, shared_grad)


def solution(mesh):
    return jax.shard_map(
        per_device,
        mesh=mesh,
        in_specs=(
            P(("groups", "shard"), None),
            P(("groups", "shard"), None),
            P("shard", None),
            P("shard", None),
            P(),
        ),
        out_specs=(
            P(("groups", "shard"), None),
            P(("groups", "shard"), None),
            P(("groups", "shard"), None),
        ),
        check_vma=False,
    )
```

profile of v0, /device:TPU:0, one launch (start us, length us, event | category | flops | bytes accessed | tf_op | source)
XLA Modules:
  0.0 424.5 jit_solution(14927127992019022304)
XLA Ops:
  7.2 0.0 copy-start
  7.2 0.0 all-gather.5.cloned.1.call-start
  7.2 0.7 all-gather.5.cloned.1.call-update
  7.9 0.0 all-gather.3.cloned.1.call-start
  8.0 0.7 all-gather.3.cloned.1.call-update
  8.7 0.0 reduce-scatter.2.cloned.1.call-start
  8.7 4.1 copy.65
  12.8 0.0 copy-done
  12.8 0.0 copy-start.3
  12.8 2.5 copy.59
  15.3 3.9 copy.60
  19.2 0.0 copy-done.3
  19.2 2.2 gather_fusion
  21.5 29.3 %all-gather.5.cloned.1.call-done = bf16[256,2048]{1,0:T(8,128)(2,1)} async-done(((bf16[16,2048]{1,0:T(8,128)(2,1)}), bf16[256,2048]{1,0:T(8,128)(2,1)}) %all-gather.5.cloned.1.call-update) | async-done | bytes 1048592 | tf_op jit(solution)/shard_map/all_gather | solution.py:39
  50.8 2.3 copy.61
  53.1 1.7 fusion.23
  54.8 4.0 convolution_bitcast_fusion
  58.8 5.4 %copy.75 = f32[256,16,256]{0,2,1:T(8,128)} copy(f32[256,16,256]{2,1,0:T(8,128)} %convolution_bitcast_fusion) | data formatting | bytes 8388608 | tf_op jit(solution)/shard_map/reshape | solution.py:49
  64.2 62.6 %all-gather.3.cloned.1.call-done = bf16[1024,4096]{1,0:T(8,128)(2,1)} async-done(((bf16[64,4096]{1,0:T(8,128)(2,1)}), bf16[1024,4096]{1,0:T(8,128)(2,1)}) %all-gather.3.cloned.1.call-update) | async-done | bytes 8388624 | tf_op jit(solution)/shard_map/all_gather | solution.py:41
  126.9 11.9 %copy.55 = bf16[1024,4096]{0,1:T(8,128)(2,1)} copy(bf16[1024,4096]{1,0:T(8,128)(2,1)} %all-gather.3.cloned.1.call-done) | data formatting | bytes 16777216 | tf_op jit(solution)/shard_map/all_gather | solution.py:41
  138.8 7.7 %convolution_bitcast_fusion.1 = f32[256,4,1024]{2,0,1:T(8,128)} fusion(bf16[1024,4,1024]{0,2,1:T(8,128)(2,1)} %bitcast.55, bf16[32,4,8,1024]{3,2,1,0:T(8,128)(2,1)S(1)} %bitcast.56), kind=kOutput, calls=%fused_computation.30 | convolution fusion | flops 2147483648 | bytes 14680064 | tf_op jit(solution)/shard_map/dot_general | solution.py:17
  146.5 5.4 %copy.58 = f32[256,4,1024]{0,2,1:T(8,128)} copy(f32[256,4,1024]{2,0,1:T(8,128)} %convolution_bitcast_fusion.1) | data formatting | bytes 8388608 | tf_op jit(solution)/shard_map/transpose | solution.py:49
  151.9 13.5 %fusion.7 = (bf16[256,4096]{0,1:T(8,128)(2,1)}, bf16[256,4096]{0,1:T(8,128)(2,1)}) fusion(bf16[256,4096]{0,1:T(8,128)(2,1)} %copy.65, f32[256,16,256]{0,2,1:T(8,128)} %copy.75, f32[256,4,1024]{0,2,1:T(8,128)} %copy.58), kind=kLoop, calls=%fused_computation.12 | loop fusion | flops 80740352 | bytes 14680064 | tf_op jit(solution)/shard_map/convert_element_type | solution.py:53
  165.4 3.9 copy.67
  169.3 3.2 gather_fusion.1
  172.5 1.8 convolution_bitcast_fusion.2
  174.3 2.5 copy.69
  176.8 2.9 reshape_reshape.3
  179.7 9.7 %fusion.15 = f32[4,1024,1024]{2,1,0:T(8,128)} fusion(bf16[256,4,1024]{0,2,1:T(8,128)(2,1)} %bitcast.59, bf16[32,4,8,1024]{3,2,1,0:T(8,128)(2,1)S(1)} %bitcast.57), kind=kOutput, calls=%fused_computation.31 | convolution fusion | flops 2147483648 | bytes 20971520 | tf_op jit(solution)/shard_map/dot_general | solution.py:62
  189.4 0.0 copy-start.2
  189.4 17.6 %copy.70 = f32[1024,4096]{1,0:T(8,128)} copy(f32[1024,4096]{0,1:T(8,128)} %bitcast.54) | data formatting | bytes 33554432 | tf_op jit(solution)/shard_map/reshape | solution.py:68
  207.0 0.0 copy-done.2
  207.0 13.7 %pad_maximum_fusion = f32[1024,4608]{1,0:T(8,128)} fusion(f32[1024,512]{1,0:T(8,128)S(1)} %copy-done.2, f32[1024,4096]{1,0:T(8,128)} %copy.70), kind=kLoop, calls=%fused_computation.2 | loop fusion | flops 4718592 | bytes 37748736 | tf_op jit(solution)/shard_map/concatenate | solution.py:66
  220.7 0.0 copy-start.1
  220.7 0.0 reduce-scatter.2.cloned.1.call-update
  220.8 1.6 copy-done.1
  222.3 2.8 copy.71
  225.2 188.9 %reduce-scatter.2.cloned.1.call-done = f32[64,4608]{1,0:T(8,128)} async-done(((f32[1024,4608]{1,0:T(8,128)}), f32[64,4608]{1,0:T(8,128)}) %reduce-scatter.2.cloned.1.call-update) | async-done | bytes 1179664 | tf_op jit(solution)/shard_map/reduce_scatter | solution.py:65
  414.1 0.9 slice.21
  415.0 0.7 reshape.50
  415.7 2.3 slice.20
  (4 shorter events, 0.0 us)
Async XLA Ops:
  7.2 5.6 %copy-start = (bf16[256,4096]{1,0:T(8,128)(2,1)S(1)}, bf16[256,4096]{1,0:T(8,128)(2,1)}, u32[]{:S(2)}) copy-start(bf16[256,4096]{1,0:T(8,128)(2,1)} %param.7) | copy-start | bytes 6291460
  7.2 43.7 %all-gather.5.cloned.1.call-start = ((), (), s32[]{:S(2)}) async-start(), calls=%async_computation.2 | async-start | bytes 1114112 | tf_op jit(solution)/shard_map/all_gather | solution.py:39
  7.9 118.9 %all-gather.3.cloned.1.call-start = ((), (), s32[]{:S(2)}) async-start(), calls=%async_computation.1 | async-start | bytes 8912896 | tf_op jit(solution)/shard_map/all_gather | solution.py:41
  8.7 405.5 %reduce-scatter.2.cloned.1.call-start = ((), (), s32[]{:S(2)}) async-start(), calls=%async_computation.3 | async-start | bytes 20054016 | tf_op jit(solution)/shard_map/reduce_scatter | solution.py:65
  12.8 6.4 %copy-start.3 = (s32[8,2]{0,1:T(2,128)S(1)}, s32[8,2]{0,1:T(2,128)}, u32[]{:S(2)}) copy-start(s32[8,2]{0,1:T(2,128)} %param.11) | copy-start | bytes 196
  189.4 17.6 %copy-start.2 = (f32[1024,512]{1,0:T(8,128)S(1)}, f32[1024,512]{1,0:T(8,128)}, u32[]{:S(2)}) copy-start(f32[1024,512]{1,0:T(8,128)} %reshape_reshape.3) | copy-start | bytes 6291460
  220.7 1.6 copy-start.1
Sparse Core Ops, SparseCore 0:
  10.2 40.6 all-gather.4
  53.0 73.8 all-gather.2
  220.9 193.1 reduce-scatter.1
where the time goes:
time: 426 us; the launch traced here: 425 us
  waiting for transfers between devices  282 us (66%)
  local copies, waits for them, and re-layouts  76.1 us (18%)
  other arithmetic  27.2 us (6%)
  matrix products  24.9 us (6%)
  between operations  13.8 us (3%)
    reduce_scatter x1, waiting for transfers between devices, per_device(): lax.psum_scatter(jnp.concatenate([jnp.transpose(term, (1, 0, 2)).reshape(...  189 us
    all_gather x1, waiting for transfers between devices, per_device(): member_full = lax.all_gather(member_weight, 'shard', axis=0, tiled=True)  62.6 us
    all_gather x1, waiting for transfers between devices, per_device(): shared_full = lax.all_gather(shared_weight, 'shard', axis=0, tiled=True)  29.3 us
    reshape x1, local copies, waits for them, and re-layouts, per_device(): jnp.transpose(term, (1, 0, 2))  17.6 us
    concatenate x1, other arithmetic, per_device(): jnp.concatenate([jnp.transpose(term, (1, 0, 2)).reshape(lax.axis_size('sh...  13.7 us
    convert_element_type x1, other arithmetic, per_device(): (cotangent.astype(jnp.float32) * gelu_slope(hidden)).astype(jnp.bfloat16)  13.5 us
    all_gather x1, local copies, waits for them, and re-layouts, per_device(): member_full = lax.all_gather(member_weight, 'shard', axis=0, tiled=True)  11.9 us
    unnamed x11, local copies, waits for them, and re-layouts  11 us
  transfers between devices with their start and end apart: 3, of which 3 were waited for; matrix products, arithmetic and copies ran while one was open for 7% of the time, Pallas kernels for 0%

commit v1 on v0

--- a/solution.py
+++ b/solution.py
@@ -5,6 +5,12 @@
 
 ROOT_HALF = 0.7071067811865476
 INV_ROOT_TWO_PI = 0.3989422804014327
+
+
+def joined_along(parts, dim):
+    parts = jnp.moveaxis(parts, 0, dim)
+    shape = parts.shape
+    return parts.reshape(*shape[:dim], shape[dim] * shape[dim + 1], *shape[dim + 2 :])
 
 
 def gelu_slope(hidden):
@@ -36,7 +42,19 @@
     )
     feat_members = features.reshape(token_rows, members, member_width)
     feat_blocks = jnp.take(features.reshape(token_rows, grid, block), row_blocks, axis=1)
-    shared_full = lax.all_gather(shared_weight, "shard", axis=0, tiled=True)
+    size = lax.axis_size("shard")
+    pairs = [(i, (i + 1) % size) for i in range(size)]
+    back = [(b, a) for a, b in pairs]
+    lower, upper = ([], [])
+    for step in range(size - 1):
+        if step % 2 == 0:
+            lower.append(lax.ppermute(lower[-1] if lower else shared_weight, "shard", pairs))
+        else:
+            upper.append(lax.ppermute(upper[-1] if upper else shared_weight, "shard", back))
+    tiles = jnp.stack([*lower[::-1], shared_weight, *upper])
+    shift = lax.axis_index("shard") - len(lower)
+    tiles = tiles[(jnp.arange(size) - shift) % size]
+    shared_full = joined_along(tiles, 0)
     shared_blocks = shared_full.reshape(block, shared_count, block)
     member_full = lax.all_gather(member_weight, "shard", axis=0, tiled=True)
     member_out = member_product(

time: 426 us -> 405 us (0.951)
  waiting for transfers between devices: 282 us -> 211 us
  starting transfers between devices: 0.11 us -> 32.4 us
  local copies, waits for them, and re-layouts: 76.1 us -> 93.8 us
    all_gather x1, waiting for transfers between devices: 62.6 us -> 0.01 us  [per_device(): member_full = lax.all_gather(member_weight, 'shard', axis=0, tiled=True)]
    ppermute x0 -> x15, starting transfers between devices: none -> 32.3 us  [the longest x7 31.8 us: per_device(): lax.ppermute(upper[-1] if upper else shared_weight, 'shard', back)]
    all_gather x1 -> x0, waiting for transfers between devices: 29.3 us -> none  [per_device(): shared_full = lax.all_gather(shared_weight, 'shard', axis=0, tiled=True)]
    ppermute x0 -> x15, waiting for transfers between devices: none -> 21.9 us  [the longest x8 14.2 us: per_device(): lax.ppermute(lower[-1] if lower else shared_weight, 'shard', pairs)]
    unnamed x11 -> x31, local copies, waits for them, and re-layouts: 11 us -> 26.2 us
  transfers between devices with their start and end apart: 3 -> 17, of which waited for: 3 -> 11; matrix products, arithmetic and copies ran while one was open for 7% -> 12% of each run, Pallas kernels for 0% -> 0%
where the time goes in v1:
time: 405 us; the launch traced here: 403 us
  waiting for transfers between devices  211 us (52%)
  local copies, waits for them, and re-layouts  93.8 us (23%)
  starting transfers between devices  32.4 us (8%)
  other arithmetic  28 us (7%)
  matrix products  24 us (6%)
  between operations  14.1 us (3%)
    reduce_scatter x1, waiting for transfers between devices, per_device(): lax.psum_scatter(jnp.concatenate([jnp.transpose(term, (1, 0, 2)).reshape(...  188 us
    ppermute x7, starting transfers between devices, per_device(): lax.ppermute(upper[-1] if upper else shared_weight, 'shard', back)  31.8 us
    unnamed x31, local copies, waits for them, and re-layouts  26.2 us
    reshape x1, local copies, waits for them, and re-layouts, per_device(): jnp.transpose(term, (1, 0, 2))  17.7 us
    ppermute x8, waiting for transfers between devices, per_device(): lax.ppermute(lower[-1] if lower else shared_weight, 'shard', pairs)  14.2 us
    concatenate x1, other arithmetic, per_device(): jnp.concatenate([jnp.transpose(term, (1, 0, 2)).reshape(lax.axis_size('sh...  13.7 us
    convert_element_type x1, other arithmetic, per_device(): (cotangent.astype(jnp.float32) * gelu_slope(hidden)).astype(jnp.bfloat16)  13.5 us
    all_gather x1, local copies, waits for them, and re-layouts, per_device(): member_full = lax.all_gather(member_weight, 'shard', axis=0, tiled=True)  11.7 us
  transfers between devices with their start and end apart: 17, of which 11 were waited for; matrix products, arithmetic and copies ran while one was open for 12% of the time, Pallas kernels for 0%

profile of v1, /device:TPU:0, one launch (start us, length us, event | category | flops | bytes accessed | tf_op | source)
XLA Modules:
  0.0 403.4 jit_solution(1280496311878032442)
XLA Ops:
  7.2 0.7 all-gather.2.cloned.1.call-update
  8.0 0.5 collective-permute-start
  8.5 7.2 %collective-permute-done = bf16[16,2048]{1,0:T(8,128)(2,1)S(1)} collective-permute-done((bf16[16,2048]{1,0:T(8,128)(2,1)}, bf16[16,2048]{1,0:T(8,128)(2,1)S(1)}, u32[]{:S(2)}, u32[]{:S(2)}) %collective-permute-start) | collective-permute-done | bytes 65568 | tf_op jit(solution)/shard_map/ppermute | solution.py:51
  15.6 4.4 %collective-permute-start.8 = (bf16[16,2048]{1,0:T(8,128)(2,1)}, bf16[16,2048]{1,0:T(8,128)(2,1)S(1)}, u32[]{:S(2)}, u32[]{:S(2)}) collective-permute-start(bf16[16,2048]{1,0:T(8,128)(2,1)} %param.10), channel_id=1, source_target_pairs={{1,0},{2,1},{3,2},{4,3},{5,4},{6,5},{7,6},{8,7},{9,8},{10,9},{11,1... | collective-permute-start | bytes 196616 | tf_op jit(solution)/shard_map/ppermute | solution.py:53
  20.1 1.9 collective-permute-done.1
  22.0 0.8 collective-permute-done.8
  22.8 4.6 %collective-permute-start.9 = (bf16[16,2048]{1,0:T(8,128)(2,1)S(1)}, bf16[16,2048]{1,0:T(8,128)(2,1)S(1)}, u32[]{:S(2)}, u32[]{:S(2)}) collective-permute-start(bf16[16,2048]{1,0:T(8,128)(2,1)S(1)} %collective-permute-done.8), channel_id=1, source_target_pairs={{1,0},{2,1},{3,2},{4,3},{5,4},{6,5},{7,6},{8,7},{9,8},{10,9},{11,1... | collective-permute-start | bytes 196616 | tf_op jit(solution)/shard_map/ppermute | solution.py:53
  27.4 2.1 collective-permute-done.2
  29.5 0.8 compare_and_fusion
  30.2 0.3 collective-permute-done.9
  30.5 4.6 %collective-permute-start.10 = (bf16[16,2048]{1,0:T(8,128)(2,1)S(1)}, bf16[16,2048]{1,0:T(8,128)(2,1)}, u32[]{:S(2)}, u32[]{:S(2)}) collective-permute-start(bf16[16,2048]{1,0:T(8,128)(2,1)S(1)} %collective-permute-done.9), channel_id=1, source_target_pairs={{1,0},{2,1},{3,2},{4,3},{5,4},{6,5},{7,6},{8,7},{9,8},{10,9},{11,1... | collective-permute-start | bytes 196616 | tf_op jit(solution)/shard_map/ppermute | solution.py:53
  35.2 2.1 collective-permute-done.3
  37.2 1.3 slice_bitcast_fusion
  38.5 4.1 %copy.48 = bf16[256,4096]{0,1:T(8,128)(2,1)} copy(bf16[256,4096]{1,0:T(8,128)(2,1)} %param.8) | data formatting | bytes 4194304 | tf_op args[1]
  42.6 2.5 copy.43
  45.1 4.0 copy.44
  49.1 4.4 %collective-permute-start.11 = (bf16[16,2048]{1,0:T(8,128)(2,1)}, bf16[16,2048]{1,0:T(8,128)(2,1)}, u32[]{:S(2)}, u32[]{:S(2)}) collective-permute-start(bf16[16,2048]{1,0:T(8,128)(2,1)} %collective-permute-done.10), channel_id=1, source_target_pairs={{1,0},{2,1},{3,2},{4,3},{5,4},{6,5},{7,6},{8,7},{9,8},{10,9},{11,1... | collective-permute-start | bytes 196616 | tf_op jit(solution)/shard_map/ppermute | solution.py:53
  53.5 2.2 gather_fusion.1
  55.7 1.3 collective-permute-done.11
  57.0 4.7 %collective-permute-start.12 = (bf16[16,2048]{1,0:T(8,128)(2,1)}, bf16[16,2048]{1,0:T(8,128)(2,1)S(1)}, u32[]{:S(2)}, u32[]{:S(2)}) collective-permute-start(bf16[16,2048]{1,0:T(8,128)(2,1)} %collective-permute-done.11), channel_id=1, source_target_pairs={{1,0},{2,1},{3,2},{4,3},{5,4},{6,5},{7,6},{8,7},{9,8},{10,9},{11,1... | collective-permute-start | bytes 196616 | tf_op jit(solution)/shard_map/ppermute | solution.py:53
  61.7 3.5 collective-permute-done.12
  65.1 4.5 %collective-permute-start.13 = (bf16[16,2048]{1,0:T(8,128)(2,1)S(1)}, bf16[16,2048]{1,0:T(8,128)(2,1)S(1)}, u32[]{:S(2)}, u32[]{:S(2)}) collective-permute-start(bf16[16,2048]{1,0:T(8,128)(2,1)S(1)} %collective-permute-done.12), channel_id=1, source_target_pairs={{1,0},{2,1},{3,2},{4,3},{5,4},{6,5},{7,6},{8,7},{9,8},{10,9},{11,1... | collective-permute-start | bytes 196616 | tf_op jit(solution)/shard_map/ppermute | solution.py:53
  69.6 1.9 collective-permute-done.13
  71.5 4.6 %collective-permute-start.14 = (bf16[16,2048]{1,0:T(8,128)(2,1)S(1)}, bf16[16,2048]{1,0:T(8,128)(2,1)S(1)}, u32[]{:S(2)}, u32[]{:S(2)}) collective-permute-start(bf16[16,2048]{1,0:T(8,128)(2,1)S(1)} %collective-permute-done.13), channel_id=1, source_target_pairs={{1,0},{2,1},{3,2},{4,3},{5,4},{6,5},{7,6},{8,7},{9,8},{10,9},{11,1... | collective-permute-start | bytes 196616 | tf_op jit(solution)/shard_map/ppermute | solution.py:53
  76.1 0.9 collective-permute-done.7
  77.0 0.6 bitcast_dynamic-update-slice_fusion.15
  77.7 0.6 bitcast_dynamic-update-slice_fusion.14
  78.3 1.5 bitcast_dynamic-update-slice_fusion.13
  79.8 1.5 bitcast_dynamic-update-slice_fusion.12
  81.3 1.5 bitcast_dynamic-update-slice_fusion.11
  82.7 0.6 bitcast_dynamic-update-slice_fusion.10
  83.4 0.6 bitcast_dynamic-update-slice_fusion.9
  84.0 0.6 bitcast_dynamic-update-slice_fusion.8
  84.6 0.6 bitcast_dynamic-update-slice_fusion.7
  85.3 0.6 bitcast_dynamic-update-slice_fusion.6
  85.9 0.6 bitcast_dynamic-update-slice_fusion.5
  86.5 1.5 bitcast_dynamic-update-slice_fusion.4
  88.0 1.5 bitcast_dynamic-update-slice_fusion.3
  89.5 0.6 bitcast_dynamic-update-slice_fusion.2
  90.1 0.6 bitcast_dynamic-update-slice_fusion.1
  90.8 0.6 bitcast_dynamic-update-slice_fusion
  91.4 3.0 gather_fusion
  94.4 1.5 copy.59
  95.9 0.5 fusion.23
  96.4 4.2 %convolution_bitcast_fusion = f32[256,16,256]{2,1,0:T(8,128)} fusion(f32[8,256,256]{2,1,0:T(8,128)S(1)} %fusion.23, s32[8]{0:T(128)S(1)} %copy-done.5), kind=kOutput, calls=%fused_computation.30 | convolution fusion | flops 100663424 | bytes 6291488 | tf_op jit(solution)/shard_map/stj,sk->tkj/dot_general | solution.py:66
  100.6 5.2 %copy.57 = f32[256,16,256]{0,2,1:T(8,128)} copy(f32[256,16,256]{2,1,0:T(8,128)} %convolution_bitcast_fusion) | data formatting | bytes 8388608 | tf_op jit(solution)/shard_map/reshape | solution.py:67
  105.9 11.7 %copy.39 = bf16[1024,4096]{0,1:T(8,128)(2,1)} copy(bf16[1024,4096]{1,0:T(8,128)(2,1)} %all-gather.2.cloned.1.call-done) | data formatting | bytes 16777216 | tf_op jit(solution)/shard_map/all_gather | solution.py:59
  117.6 7.8 %convolution_bitcast_fusion.1 = f32[256,4,1024]{2,0,1:T(8,128)} fusion(bf16[1024,4,1024]{0,2,1:T(8,128)(2,1)} %bitcast.90, bf16[32,4,8,1024]{3,2,1,0:T(8,128)(2,1)S(1)} %bitcast.91), kind=kOutput, calls=%fused_computation.31 | convolution fusion | flops 2147483648 | bytes 14680064 | tf_op jit(solution)/shard_map/dot_general | solution.py:23
  125.4 5.4 %copy.42 = f32[256,4,1024]{0,2,1:T(8,128)} copy(f32[256,4,1024]{2,0,1:T(8,128)} %convolution_bitcast_fusion.1) | data formatting | bytes 8388608 | tf_op jit(solution)/shard_map/transpose | solution.py:67
  130.8 13.5 %fusion.7 = (bf16[256,4096]{0,1:T(8,128)(2,1)}, bf16[256,4096]{0,1:T(8,128)(2,1)}) fusion(bf16[256,4096]{0,1:T(8,128)(2,1)} %copy.48, f32[256,16,256]{0,2,1:T(8,128)} %copy.57, f32[256,4,1024]{0,2,1:T(8,128)} %copy.42), kind=kLoop, calls=%fused_computation.13 | loop fusion | flops 80740352 | bytes 14680064 | tf_op jit(solution)/shard_map/convert_element_type | solution.py:71
  144.3 3.9 copy.50
  148.2 3.2 gather_fusion.2
  151.4 1.8 convolution_bitcast_fusion.2
  153.2 2.5 copy.52
  155.7 2.9 reshape_reshape.7
  158.6 9.7 %fusion.15 = f32[4,1024,1024]{2,1,0:T(8,128)} fusion(bf16[256,4,1024]{0,2,1:T(8,128)(2,1)} %bitcast.94, bf16[32,4,8,1024]{3,2,1,0:T(8,128)(2,1)S(1)} %bitcast.92), kind=kOutput, calls=%fused_computation.32 | convolution fusion | flops 2147483648 | bytes 20971520 | tf_op jit(solution)/shard_map/dot_general | solution.py:80
  168.3 17.7 %copy.53 = f32[1024,4096]{1,0:T(8,128)} copy(f32[1024,4096]{0,1:T(8,128)} %bitcast.89) | data formatting | bytes 33554432 | tf_op jit(solution)/shard_map/reshape | solution.py:86
  186.0 13.7 %pad_maximum_fusion = f32[1024,4608]{1,0:T(8,128)} fusion(f32[1024,512]{1,0:T(8,128)S(1)} %copy-done.2, f32[1024,4096]{1,0:T(8,128)} %copy.53), kind=kLoop, calls=%fused_computation.3 | loop fusion | flops 4718592 | bytes 37748736 | tf_op jit(solution)/shard_map/concatenate | solution.py:84
  199.7 1.6 copy-done.1
  201.3 2.8 copy.54
  204.2 188.5 %reduce-scatter.2.cloned.1.call-done = f32[64,4608]{1,0:T(8,128)} async-done(((f32[1024,4608]{1,0:T(8,128)}), f32[64,4608]{1,0:T(8,128)}) %reduce-scatter.2.cloned.1.call-update) | async-done | bytes 1179664 | tf_op jit(solution)/shard_map/reduce_scatter | solution.py:83
  392.6 0.9 slice.23
  393.5 0.7 reshape.95
  394.3 2.3 slice.22
  (30 shorter events, 0.2 us)
Async XLA Ops:
  7.2 35.4 %copy-start = (bf16[256,4096]{1,0:T(8,128)(2,1)S(1)}, bf16[256,4096]{1,0:T(8,128)(2,1)}, u32[]{:S(2)}) copy-start(bf16[256,4096]{1,0:T(8,128)(2,1)} %param.7) | copy-start | bytes 6291460
  7.2 98.7 %all-gather.2.cloned.1.call-start = ((), (), s32[]{:S(2)}) async-start(), calls=%async_computation.1 | async-start | bytes 8912896 | tf_op jit(solution)/shard_map/all_gather | solution.py:59
  7.9 384.7 %reduce-scatter.2.cloned.1.call-start = ((), (), s32[]{:S(2)}) async-start(), calls=%async_computation.2 | async-start | bytes 20054016 | tf_op jit(solution)/shard_map/reduce_scatter | solution.py:83
  8.0 7.7 %collective-permute-start = (bf16[16,2048]{1,0:T(8,128)(2,1)}, bf16[16,2048]{1,0:T(8,128)(2,1)S(1)}, u32[]{:S(2)}, u32[]{:S(2)}) collective-permute-start(bf16[16,2048]{1,0:T(8,128)(2,1)} %param.10), channel_id=1, source_target_pairs={{0,1},{1,2},{2,3},{3,4},{4,5},{5,6},{6,7},{7,8},{8,9},{9,10},{10,1... | collective-permute-start | bytes 196616 | tf_op jit(solution)/shard_map/ppermute | solution.py:51
  15.6 6.4 %collective-permute-start.1 = (bf16[16,2048]{1,0:T(8,128)(2,1)S(1)}, bf16[16,2048]{1,0:T(8,128)(2,1)S(1)}, u32[]{:S(2)}, u32[]{:S(2)}) collective-permute-start(bf16[16,2048]{1,0:T(8,128)(2,1)S(1)} %collective-permute-done), channel_id=1, source_target_pairs={{0,1},{1,2},{2,3},{3,4},{4,5},{5,6},{6,7},{7,8},{8,9},{9,10},{10,1... | collective-permute-start | bytes 196616 | tf_op jit(solution)/shard_map/ppermute | solution.py:51
  15.6 7.2 %collective-permute-start.8 = (bf16[16,2048]{1,0:T(8,128)(2,1)}, bf16[16,2048]{1,0:T(8,128)(2,1)S(1)}, u32[]{:S(2)}, u32[]{:S(2)}) collective-permute-start(bf16[16,2048]{1,0:T(8,128)(2,1)} %param.10), channel_id=1, source_target_pairs={{1,0},{2,1},{3,2},{4,3},{5,4},{6,5},{7,6},{8,7},{9,8},{10,9},{11,1... | collective-permute-start | bytes 196616 | tf_op jit(solution)/shard_map/ppermute | solution.py:53
  22.0 7.5 %collective-permute-start.2 = (bf16[16,2048]{1,0:T(8,128)(2,1)S(1)}, bf16[16,2048]{1,0:T(8,128)(2,1)S(1)}, u32[]{:S(2)}, u32[]{:S(2)}) collective-permute-start(bf16[16,2048]{1,0:T(8,128)(2,1)S(1)} %collective-permute-done.1), channel_id=1, source_target_pairs={{0,1},{1,2},{2,3},{3,4},{4,5},{5,6},{6,7},{7,8},{8,9},{9,10},{10,1... | collective-permute-start | bytes 196616 | tf_op jit(solution)/shard_map/ppermute | solution.py:51
  22.8 7.7 %collective-permute-start.9 = (bf16[16,2048]{1,0:T(8,128)(2,1)S(1)}, bf16[16,2048]{1,0:T(8,128)(2,1)S(1)}, u32[]{:S(2)}, u32[]{:S(2)}) collective-permute-start(bf16[16,2048]{1,0:T(8,128)(2,1)S(1)} %collective-permute-done.8), channel_id=1, source_target_pairs={{1,0},{2,1},{3,2},{4,3},{5,4},{6,5},{7,6},{8,7},{9,8},{10,9},{11,1... | collective-permute-start | bytes 196616 | tf_op jit(solution)/shard_map/ppermute | solution.py:53
  29.5 7.8 %collective-permute-start.3 = (bf16[16,2048]{1,0:T(8,128)(2,1)S(1)}, bf16[16,2048]{1,0:T(8,128)(2,1)S(1)}, u32[]{:S(2)}, u32[]{:S(2)}) collective-permute-start(bf16[16,2048]{1,0:T(8,128)(2,1)S(1)} %collective-permute-done.2), channel_id=1, source_target_pairs={{0,1},{1,2},{2,3},{3,4},{4,5},{5,6},{6,7},{7,8},{8,9},{9,10},{10,1... | collective-permute-start | bytes 196616 | tf_op jit(solution)/shard_map/ppermute | solution.py:51
  30.5 18.5 %collective-permute-start.10 = (bf16[16,2048]{1,0:T(8,128)(2,1)S(1)}, bf16[16,2048]{1,0:T(8,128)(2,1)}, u32[]{:S(2)}, u32[]{:S(2)}) collective-permute-start(bf16[16,2048]{1,0:T(8,128)(2,1)S(1)} %collective-permute-done.9), channel_id=1, source_target_pairs={{1,0},{2,1},{3,2},{4,3},{5,4},{6,5},{7,6},{8,7},{9,8},{10,9},{11,1... | collective-permute-start | bytes 196616 | tf_op jit(solution)/shard_map/ppermute | solution.py:53
  37.2 7.9 %copy-start.4 = (bf16[16,2048]{1,0:T(8,128)(2,1)}, bf16[16,2048]{1,0:T(8,128)(2,1)S(1)}, u32[]{:S(2)}) copy-start(bf16[16,2048]{1,0:T(8,128)(2,1)S(1)} %collective-permute-done.3) | copy-start | bytes 196612
  37.2 16.2 %collective-permute-start.4 = (bf16[16,2048]{1,0:T(8,128)(2,1)S(1)}, bf16[16,2048]{1,0:T(8,128)(2,1)}, u32[]{:S(2)}, u32[]{:S(2)}) collective-permute-start(bf16[16,2048]{1,0:T(8,128)(2,1)S(1)} %collective-permute-done.3), channel_id=1, source_target_pairs={{0,1},{1,2},{2,3},{3,4},{4,5},{5,6},{6,7},{7,8},{8,9},{9,10},{10,1... | collective-permute-start | bytes 196616 | tf_op jit(solution)/shard_map/ppermute | solution.py:51
  45.1 39.5 %copy-start.3 = (bf16[16,2048]{1,0:T(8,128)(2,1)S(1)}, bf16[16,2048]{1,0:T(8,128)(2,1)}, u32[]{:S(2)}) copy-start(bf16[16,2048]{1,0:T(8,128)(2,1)} %param.10) | copy-start | bytes 196612
  49.1 7.9 %collective-permute-start.11 = (bf16[16,2048]{1,0:T(8,128)(2,1)}, bf16[16,2048]{1,0:T(8,128)(2,1)}, u32[]{:S(2)}, u32[]{:S(2)}) collective-permute-start(bf16[16,2048]{1,0:T(8,128)(2,1)} %collective-permute-done.10), channel_id=1, source_target_pairs={{1,0},{2,1},{3,2},{4,3},{5,4},{6,5},{7,6},{8,7},{9,8},{10,9},{11,1... | collective-permute-start | bytes 196616 | tf_op jit(solution)/shard_map/ppermute | solution.py:53
  53.5 8.2 %collective-permute-start.5 = (bf16[16,2048]{1,0:T(8,128)(2,1)}, bf16[16,2048]{1,0:T(8,128)(2,1)}, u32[]{:S(2)}, u32[]{:S(2)}) collective-permute-start(bf16[16,2048]{1,0:T(8,128)(2,1)} %collective-permute-done.4), channel_id=1, source_target_pairs={{0,1},{1,2},{2,3},{3,4},{4,5},{5,6},{6,7},{7,8},{8,9},{9,10},{10,1... | collective-permute-start | bytes 196616 | tf_op jit(solution)/shard_map/ppermute | solution.py:51
  57.0 8.1 %collective-permute-start.12 = (bf16[16,2048]{1,0:T(8,128)(2,1)}, bf16[16,2048]{1,0:T(8,128)(2,1)S(1)}, u32[]{:S(2)}, u32[]{:S(2)}) collective-permute-start(bf16[16,2048]{1,0:T(8,128)(2,1)} %collective-permute-done.11), channel_id=1, source_target_pairs={{1,0},{2,1},{3,2},{4,3},{5,4},{6,5},{7,6},{8,7},{9,8},{10,9},{11,1... | collective-permute-start | bytes 196616 | tf_op jit(solution)/shard_map/ppermute | solution.py:53
  61.7 8.0 %collective-permute-start.6 = (bf16[16,2048]{1,0:T(8,128)(2,1)}, bf16[16,2048]{1,0:T(8,128)(2,1)S(1)}, u32[]{:S(2)}, u32[]{:S(2)}) collective-permute-start(bf16[16,2048]{1,0:T(8,128)(2,1)} %collective-permute-done.5), channel_id=1, source_target_pairs={{0,1},{1,2},{2,3},{3,4},{4,5},{5,6},{6,7},{7,8},{8,9},{9,10},{10,1... | collective-permute-start | bytes 196616 | tf_op jit(solution)/shard_map/ppermute | solution.py:51
  65.1 6.4 %collective-permute-start.13 = (bf16[16,2048]{1,0:T(8,128)(2,1)S(1)}, bf16[16,2048]{1,0:T(8,128)(2,1)S(1)}, u32[]{:S(2)}, u32[]{:S(2)}) collective-permute-start(bf16[16,2048]{1,0:T(8,128)(2,1)S(1)} %collective-permute-done.12), channel_id=1, source_target_pairs={{1,0},{2,1},{3,2},{4,3},{5,4},{6,5},{7,6},{8,7},{9,8},{10,9},{11,1... | collective-permute-start | bytes 196616 | tf_op jit(solution)/shard_map/ppermute | solution.py:53
  69.6 7.4 %collective-permute-start.7 = (bf16[16,2048]{1,0:T(8,128)(2,1)S(1)}, bf16[16,2048]{1,0:T(8,128)(2,1)S(1)}, u32[]{:S(2)}, u32[]{:S(2)}) collective-permute-start(bf16[16,2048]{1,0:T(8,128)(2,1)S(1)} %collective-permute-done.6), channel_id=1, source_target_pairs={{0,1},{1,2},{2,3},{3,4},{4,5},{5,6},{6,7},{7,8},{8,9},{9,10},{10,1... | collective-permute-start | bytes 196616 | tf_op jit(solution)/shard_map/ppermute | solution.py:51
  71.5 19.2 %collective-permute-start.14 = (bf16[16,2048]{1,0:T(8,128)(2,1)S(1)}, bf16[16,2048]{1,0:T(8,128)(2,1)S(1)}, u32[]{:S(2)}, u32[]{:S(2)}) collective-permute-start(bf16[16,2048]{1,0:T(8,128)(2,1)S(1)} %collective-permute-done.13), channel_id=1, source_target_pairs={{1,0},{2,1},{3,2},{4,3},{5,4},{6,5},{7,6},{8,7},{9,8},{10,9},{11,1... | collective-permute-start | bytes 196616 | tf_op jit(solution)/shard_map/ppermute | solution.py:53
  91.4 5.0 %copy-start.5 = (s32[8]{0:T(128)S(1)}, s32[8]{0:T(128)}, u32[]{:S(2)}) copy-start(s32[8]{0:T(128)} %slice_bitcast_fusion) | copy-start | bytes 100
  168.3 17.7 %copy-start.2 = (f32[1024,512]{1,0:T(8,128)S(1)}, f32[1024,512]{1,0:T(8,128)}, u32[]{:S(2)}) copy-start(f32[1024,512]{1,0:T(8,128)} %reshape_reshape.7) | copy-start | bytes 6291460
  199.7 1.6 copy-start.1
Sparse Core Ops, SparseCore 0:
  10.2 82.8 all-gather.1
  199.9 192.7 reduce-scatter.1
